TPU v7x, 256 devices: a whole 4x4x8 slice. The times are simulated.
256 devices in a mesh: dp: 32 (over x, y, core), mp: 8 (over z).
Axes of the slice: x: 4, y: 4, z: 8, core: 2. Of those that a mesh axis runs over, the one named last changes fastest.
Arguments:
- queries: bfloat16 [4096, 64, 128], P('dp', 'mp'), may hold values from -6 to 6
- key_cache: bfloat16 [4096, 8, 128, 128], P('dp', 'mp'), may hold values from -6 to 6
- value_cache: bfloat16 [4096, 8, 128, 128], P('dp', 'mp'), may hold values from -6 to 6
- key_new: bfloat16 [4096, 8, 128], P('dp', 'mp'), may hold values from -6 to 6
- value_new: bfloat16 [4096, 8, 128], P('dp', 'mp'), may hold values from -6 to 6
- lengths: int32 [4096], P('dp'), may hold values from 1 to 128, as said below
- occupied: int32 [4096], P('dp'), may hold values 0 or 1
- slot_request: int32 [4096], P('dp'), may hold values from 0 to 4095, as said below
- request_adapter: int32 [4096], replicated, may hold values from 0 to 63, as said below
- out_weight: bfloat16 [8192, 4096], P('mp'), may hold values from -0.375 to 0.375
- shrink_weight: bfloat16 [64, 8192, 64], P('dp', 'mp'), may hold values from -0.375 to 0.375
- expand_weight: bfloat16 [64, 64, 4096], P('dp', None, 'mp'), may hold values from -0.75 to 0.75
Outputs:
- mixed: bfloat16 [4096, 4096], P('dp', 'mp')
Inputs may be any that keep to these rules, and one draw needn't show every extreme that they name: `slot_request`: A permutation: each request stands in exactly one slot. `request_adapter`: adapter n is owned by dp index n // 2. Among the slots of one dp index, at most 8 hold requests whose adapters one dp index owns; in every draw some dp index owns the adapters of exactly 8 slots of every dp index. `lengths`: each dp index has a slot of length 128.
All inputs are finite; a program needn't handle non-finite values. No bound on the sum of `occupied` on one device may be relied on, other than what follows from the above.
Results may differ from a plain program's by a relative error of at most 0.011.
Values may be sent and summed in bfloat16 or wider, within the bound.
A program may use at most 64 MiB of HBM per device.

v0:
```python
import math
import jax
import jax.numpy as jnp
from jax import lax
from jax.sharding import PartitionSpec as P


def attend(queries, key_cache, value_cache, key_new, value_new, lengths):
    rows, heads, width = queries.shape
    kv_local = key_cache.shape[1]
    group = heads // kv_local
    inverse = 1.0 / math.sqrt(width)
    grouped = queries.reshape(rows, kv_local, group, width)
    cached = (
        jnp.einsum("bgjd,bgtd->bgjt", grouped, key_cache, preferred_element_type=jnp.float32)
        * inverse
    )
    fresh = (
        jnp.einsum("bgjd,bgd->bgj", grouped, key_new, preferred_element_type=jnp.float32) * inverse
    )
    valid = jnp.arange(key_cache.shape[2])[None, :] < lengths[:, None]
    cached = jnp.where(valid[:, None, None, :], cached, -jnp.inf)
    top = jnp.maximum(jnp.max(cached, axis=-1), fresh)
    cached_exp = jnp.exp(cached - top[..., None])
    fresh_exp = jnp.exp(fresh - top)
    total = jnp.sum(cached_exp, axis=-1) + fresh_exp
    cached_w = (cached_exp / total[..., None]).astype(jnp.bfloat16)
    fresh_w = (fresh_exp / total).astype(jnp.bfloat16)
    summed = jnp.einsum(
        "bgjt,bgtd->bgjd", cached_w, value_cache, preferred_element_type=jnp.float32
    )
    summed = (
        summed
        + fresh_w.astype(jnp.float32)[..., None] * value_new.astype(jnp.float32)[:, :, None, :]
    )
    return summed.reshape(rows, heads * width).astype(jnp.bfloat16)


def body(
    queries,
    key_cache,
    value_cache,
    key_new,
    value_new,
    lengths,
    occupied,
    slot_request,
    request_adapter,
    out_weight,
    shrink_weight,
    expand_weight,
):
    rows = queries.shape[0]
    attended = attend(queries, key_cache, value_cache, key_new, value_new, lengths)
    owners_count = lax.axis_size("dp")
    adapters_here = shrink_weight.shape[0]
    rank_width = shrink_weight.shape[2]
    out_local = expand_weight.shape[2]
    capacity = 2 * rows // owners_count
    matches = (
        slot_request[:, None] == jnp.arange(request_adapter.shape[0], dtype=jnp.int32)[None, :]
    )
    slot_adapter = jnp.sum(jnp.where(matches, request_adapter[None, :], 0), axis=1)
    owner = slot_adapter // adapters_here
    local_ids = slot_adapter % adapters_here
    owner_onehot = (owner[:, None] == jnp.arange(owners_count, dtype=jnp.int32)[None, :]).astype(
        jnp.int32
    )
    earlier = jnp.cumsum(owner_onehot, axis=0) - owner_onehot
    position = jnp.sum(earlier * owner_onehot, axis=1)
    slot_code = owner * capacity + position
    dispatch = jnp.arange(owners_count * capacity, dtype=jnp.int32)[:, None] == slot_code[None, :]
    send_rows = jnp.dot(
        dispatch.astype(jnp.bfloat16), attended, preferred_element_type=jnp.float32
    ).astype(jnp.bfloat16)
    send_rows = send_rows.reshape(owners_count, capacity, attended.shape[1])
    send_ids = jnp.sum(jnp.where(dispatch, (local_ids + 1)[None, :], 0), axis=1).reshape(
        owners_count, capacity
    )
    combine = (
        slot_code[:, None] == jnp.arange(owners_count * capacity, dtype=jnp.int32)[None, :]
    ).astype(jnp.bfloat16)
    partial_value = jnp.dot(attended, out_weight, preferred_element_type=jnp.float32)
    full = lax.psum(partial_value, "mp")
    base = lax.dynamic_slice_in_dim(full, lax.axis_index("mp") * out_local, out_local, 1)
    got_rows = lax.all_to_all(send_rows, "dp", split_axis=0, concat_axis=0, tiled=True)
    got_ids = lax.all_to_all(send_ids, "dp", split_axis=0, concat_axis=0, tiled=True)
    flat = got_rows.reshape(owners_count * capacity, got_rows.shape[2])
    wanted = got_ids.reshape(owners_count * capacity) - 1
    partial_value = jnp.einsum(
        "md,adr->mar", flat, shrink_weight, preferred_element_type=jnp.float32
    )
    which = jnp.arange(adapters_here, dtype=jnp.int32)[None, :] == wanted[:, None]
    partial_value = jnp.where(which[:, :, None], partial_value, 0.0)
    summed = lax.psum(
        partial_value.reshape(owners_count * capacity, adapters_here * rank_width), "mp"
    )
    low = summed.astype(jnp.bfloat16).reshape(owners_count * capacity, adapters_here, rank_width)
    delta = 0.5 * jnp.einsum("mar,are->me", low, expand_weight, preferred_element_type=jnp.float32)
    delta = delta.astype(jnp.bfloat16).reshape(owners_count, capacity, out_local)
    back = lax.all_to_all(delta, "dp", split_axis=0, concat_axis=0, tiled=True)
    correction = jnp.dot(
        combine,
        back.reshape(owners_count * capacity, out_local),
        preferred_element_type=jnp.float32,
    )
    return (occupied.astype(jnp.float32)[:, None] * (base + correction)).astype(jnp.bfloat16)


def solution(mesh):
    placed = (
        P("dp", "mp", None),
        P("dp", "mp", None, None),
        P("dp", "mp", None, None),
        P("dp", "mp", None),
        P("dp", "mp", None),
        P("dp"),
        P("dp"),
        P("dp"),
        P(),
        P("mp", None),
        P("dp", "mp", None),
        P("dp", None, "mp"),
    )
    return jax.shard_map(body, mesh=mesh, in_specs=placed, out_specs=P("dp", "mp"), check_vma=False)
```

profile of v0, /device:TPU:22, one launch (start us, length us, event | category | flops | bytes accessed | tf_op | source)
XLA Modules:
  0.0 117.1 jit_solution(17132844115245272164)
XLA Ops:
  6.5 0.0 copy-start
  6.5 0.0 copy-start.1
  6.5 0.0 copy-start.6
  6.5 0.0 copy-start.3
  6.5 0.0 all-reduce.3.cloned.1.call-start
  6.6 0.8 iota_compare_fusion.6
  7.4 4.6 %fusion.42 = (f32[128,8]{1,0:T(8,128)S(1)}, f32[128,8,128]{2,1,0:T(8,128)S(1)}) fusion(bf16[128,8,128]{2,1,0:T(8,128)(2,1)} %param.12, bf16[128,1,128,128]{3,2,1,0:T(8,128)(2,1)} %param.13, pred[128,128]{1,0:T(8,128)(4,1)S(1)} %iota_compare_fusion.6), kind=kOutput, calls=%fused_computation.60 | convolution fusion | flops 33946624 | bytes 5001216 | tf_op jit(solution)/shard_map/bgjd,bgtd->bgjt/dot_general | solution.py:15
  12.0 0.1 copy.19
  12.1 0.0 copy-done.1
  12.1 0.0 copy-done.6
  12.1 0.3 fusion.36
  12.4 0.1 copy.20
  12.6 0.4 fusion.24
  13.0 0.1 copy.22
  13.1 0.1 copy.23
  13.2 0.0 copy-done.3
  13.3 3.5 %fusion.16 = bf16[128,8,128]{2,1,0:T(8,128)(2,1)S(1)} fusion(bf16[128,1,128,128]{3,2,1,0:T(8,128)(2,1)} %param.14, f32[128,8,128]{2,1,0:T(8,128)S(1)} %get-tuple-element.10, f32[128,128]{1,0:T(8,128)S(1)} %bitcast_convert_fusion, f32[128,8]{1,0:T(8,128)S(1)} %copy.23, f32[128,8]{1,0:T(8,128)S(1)} %copy.22, f32[128,8]{1,0:T(8,128)S(1)} %copy.20), kind=kOutput, calls=%fused_computation.14 | convolution fusion | flops 34340864 | bytes 5058560 | tf_op jit(solution)/shard_map/bgjt,bgtd->bgjd/dot_general | solution.py:29
  16.7 0.0 copy-start.4
  16.7 0.0 copy-start.5
  16.7 6.0 %fusion.26 = f32[128,4096]{1,0:T(8,128)} fusion(bf16[1024,4096]{1,0:T(8,128)(2,1)} %param.21, bf16[16,8,8,128]{3,2,1,0:T(8,128)(2,1)S(1)} %bitcast.75), kind=kOutput, calls=%fused_computation.25 | convolution fusion | flops 1073741824 | bytes 10747904 | tf_op jit(solution)/shard_map/dot_general | solution.py:83
  22.7 0.0 copy-start.2
  22.7 0.0 copy-start.7
  22.7 0.0 all-reduce.3.cloned.1.call-update
  22.7 0.0 copy-done.4
  22.8 0.0 copy-done.5
  22.8 0.4 select_reduce_fusion
  23.2 0.1 fusion.35
  23.3 0.2 reduce_window_sum.11
  23.5 0.2 select_reduce_fusion.2
  23.7 0.1 select_reduce_fusion.1
  23.8 0.7 all_to_all.12
  24.5 7.4 %all-to-all-start = ((s32[32,1,8]{2,1,0:T(1,128)}), s32[32,1,8]{2,1,0:T(1,128)S(1)}, u32[]{:S(2)}, u32[]{:S(2)}) async-start(s32[32,1,8]{2,1,0:T(1,128)} %bitcast.6), calls=%async_computation | async-start | bytes 32768 | tf_op jit(solution)/shard_map/all_to_all | solution.py:87
  31.9 1.1 fusion.4
  33.0 2.5 %all-to-all-done = s32[32,1,8]{2,1,0:T(1,128)S(1)} async-done(((s32[32,1,8]{2,1,0:T(1,128)}), s32[32,1,8]{2,1,0:T(1,128)S(1)}, u32[]{:S(2)}, u32[]{:S(2)}) %all-to-all-start) | async-done | bytes 1056 | tf_op jit(solution)/shard_map/all_to_all | solution.py:87
  35.4 7.6 %all-to-all-start.1 = ((bf16[32,8,1024]{2,1,0:T(8,128)(2,1)}), bf16[32,8,1024]{2,1,0:T(8,128)(2,1)S(1)}, u32[]{:S(2)}, u32[]{:S(2)}) async-start(bf16[32,8,1024]{2,1,0:T(8,128)(2,1)} %fusion.4), calls=%async_computation.1 | async-start | bytes 1048576 | tf_op jit(solution)/shard_map/all_to_all | solution.py:86
  43.1 0.1 sub.34
  43.2 7.9 %all-to-all-done.1 = bf16[32,8,1024]{2,1,0:T(8,128)(2,1)S(1)} async-done(((bf16[32,8,1024]{2,1,0:T(8,128)(2,1)}), bf16[32,8,1024]{2,1,0:T(8,128)(2,1)S(1)}, u32[]{:S(2)}, u32[]{:S(2)}) %all-to-all-start.1) | async-done | bytes 524320 | tf_op jit(solution)/shard_map/all_to_all | solution.py:86
  51.1 0.0 copy-done
  51.1 0.3 fusion.22
  51.5 34.2 %all-reduce.4 = bf16[256,128]{0,1:T(8,128)(2,1)S(1)} all-reduce(f32[256,128]{0,1:T(8,128)S(1)} %bitcast.78), channel_id=1, replica_groups=mesh['dp'=32,'mp'=8] {'mp'}, use_global_device_ids=true, to_apply=%region_7.8 | all-reduce | flops 32768 | bytes 196608 | tf_op jit(solution)/shard_map/psum | solution.py:95
  85.7 0.0 copy-done.2
  85.7 0.9 fusion.19
  86.6 7.1 %all-to-all-start.2 = ((bf16[32,8,512]{2,1,0:T(8,128)(2,1)}), bf16[32,8,512]{2,1,0:T(8,128)(2,1)S(1)}, u32[]{:S(2)}, u32[]{:S(2)}) async-start(bf16[32,8,512]{2,1,0:T(8,128)(2,1)} %fusion.19), calls=%async_computation.2 | async-start | bytes 524288 | tf_op jit(solution)/shard_map/all_to_all | solution.py:101
  93.8 0.0 copy-done.7
  93.8 5.3 %all-to-all-done.2 = bf16[32,8,512]{2,1,0:T(8,128)(2,1)S(1)} async-done(((bf16[32,8,512]{2,1,0:T(8,128)(2,1)}), bf16[32,8,512]{2,1,0:T(8,128)(2,1)S(1)}, u32[]{:S(2)}, u32[]{:S(2)}) %all-to-all-start.2) | async-done | bytes 262176 | tf_op jit(solution)/shard_map/all_to_all | solution.py:101
  99.1 9.4 %all-reduce.3.cloned.1.call-done = f32[128,4096]{1,0:T(8,128)} async-done(((f32[128,4096]{1,0:T(8,128)}), f32[128,4096]{1,0:T(8,128)}) %all-reduce.3.cloned.1.call-update) | async-done | bytes 2097168 | tf_op jit(solution)/shard_map/psum | solution.py:84
  108.5 1.8 %fusion.21 = bf16[128,512]{1,0:T(8,128)(2,1)} fusion(bf16[32,8,512]{2,1,0:T(8,128)(2,1)S(1)} %all-to-all-done.2, f32[128,4096]{1,0:T(8,128)} %all-reduce.3.cloned.1.call-done, s32[]{:T(128)S(6)} %select_n.48, f32[128]{0:T(128)S(1)} %convert_element_type.39, s32[128]{0:T(128)S(1)} %multiply_add_fusion), kind=kOutput, calls=%fused_computation.18 | convolution fusion | flops 33783808 | bytes 656388 | tf_op jit(solution)/shard_map/dot_general | solution.py:102
  (11 shorter events, 0.2 us)
Async XLA Ops:
  6.5 44.6 %copy-start = (bf16[2,1024,64]{1,2,0:T(8,128)(2,1)S(1)}, bf16[2,1024,64]{1,2,0:T(8,128)(2,1)}, u32[]{:S(2)}) copy-start(bf16[2,1024,64]{1,2,0:T(8,128)(2,1)} %param.22) | copy-start | bytes 786436
  6.5 5.5 %copy-start.1 = (bf16[128,8,128]{2,1,0:T(8,128)(2,1)S(1)}, bf16[128,8,128]{2,1,0:T(8,128)(2,1)}, u32[]{:S(2)}) copy-start(bf16[128,8,128]{2,1,0:T(8,128)(2,1)} %param.12) | copy-start | bytes 786436
  6.5 5.5 %copy-start.6 = (bf16[128,1,128]{2,0,1:T(8,128)(2,1)S(1)}, bf16[128,1,128]{2,0,1:T(8,128)(2,1)}, u32[]{:S(2)}) copy-start(bf16[128,1,128]{2,0,1:T(8,128)(2,1)} %param.15) | copy-start | bytes 98308
  6.5 6.7 %copy-start.3 = (bf16[128,1,128]{2,0,1:T(8,128)(2,1)S(1)}, bf16[128,1,128]{2,0,1:T(8,128)(2,1)}, u32[]{:S(2)}) copy-start(bf16[128,1,128]{2,0,1:T(8,128)(2,1)} %param.16) | copy-start | bytes 98308
  6.5 101.9 %all-reduce.3.cloned.1.call-start = ((), (), s32[]{:S(2)}) async-start(), calls=%async_computation.3 | async-start | bytes 4194304 | tf_op jit(solution)/shard_map/psum | solution.py:84
  16.7 6.0 %copy-start.4 = (s32[4096]{0:T(1024)S(1)}, s32[4096]{0:T(1024)}, u32[]{:S(2)}) copy-start(s32[4096]{0:T(1024)} %param.20) | copy-start | bytes 49156
  16.7 6.0 %copy-start.5 = (s32[128]{0:T(128)S(1)}, s32[128]{0:T(128)}, u32[]{:S(2)}) copy-start(s32[128]{0:T(128)} %param.19) | copy-start | bytes 1540
  22.7 63.0 %copy-start.2 = (bf16[2,64,512]{2,1,0:T(8,128)(2,1)S(1)}, bf16[2,64,512]{2,1,0:T(8,128)(2,1)}, u32[]{:S(2)}) copy-start(bf16[2,64,512]{2,1,0:T(8,128)(2,1)} %param.23) | copy-start | bytes 393220
  22.7 71.1 %copy-start.7 = (s32[128]{0:T(128)S(1)}, s32[128]{0:T(128)}, u32[]{:S(2)}) copy-start(s32[128]{0:T(128)} %param.18) | copy-start | bytes 1540
  24.5 11.0 %all-to-all-start = ((s32[32,1,8]{2,1,0:T(1,128)}), s32[32,1,8]{2,1,0:T(1,128)S(1)}, u32[]{:S(2)}, u32[]{:S(2)}) async-start(s32[32,1,8]{2,1,0:T(1,128)} %bitcast.6), calls=%async_computation | async-start | bytes 32768 | tf_op jit(solution)/shard_map/all_to_all | solution.py:87
  35.4 15.7 %all-to-all-start.1 = ((bf16[32,8,1024]{2,1,0:T(8,128)(2,1)}), bf16[32,8,1024]{2,1,0:T(8,128)(2,1)S(1)}, u32[]{:S(2)}, u32[]{:S(2)}) async-start(bf16[32,8,1024]{2,1,0:T(8,128)(2,1)} %fusion.4), calls=%async_computation.1 | async-start | bytes 1048576 | tf_op jit(solution)/shard_map/all_to_all | solution.py:86
  86.6 12.4 %all-to-all-start.2 = ((bf16[32,8,512]{2,1,0:T(8,128)(2,1)}), bf16[32,8,512]{2,1,0:T(8,128)(2,1)S(1)}, u32[]{:S(2)}, u32[]{:S(2)}) async-start(bf16[32,8,512]{2,1,0:T(8,128)(2,1)} %fusion.19), calls=%async_computation.2 | async-start | bytes 524288 | tf_op jit(solution)/shard_map/all_to_all | solution.py:101
Sparse Core Ops, SparseCore 0:
  22.9 85.5 all-reduce.2
where the time goes:
time: 118 us; the launch traced here: 117 us
  blocking collectives  34.2 us (29%)
  waiting for transfers between devices  25.1 us (21%)
  starting transfers between devices  22.2 us (19%)
  matrix products  18.5 us (16%)
  between operations  13.6 us (12%)
  other arithmetic  2.26 us (2%)
  local copies, waits for them, and re-layouts  1.31 us (1%)
    psum x1, blocking collectives, body(): lax.psum(partial_value.reshape(owners_count * capacity, adapters_here * r...  34.2 us
    psum x1, waiting for transfers between devices, body(): full = lax.psum(partial_value, 'mp')  9.39 us
    all_to_all x1, waiting for transfers between devices, body(): lax.all_to_all(send_rows, 'dp', split_axis=0, concat_axis=0, tiled=True)  7.91 us
    all_to_all x1, starting transfers between devices, body(): lax.all_to_all(send_rows, 'dp', split_axis=0, concat_axis=0, tiled=True)  7.63 us
    all_to_all x1, starting transfers between devices, body(): lax.all_to_all(send_ids, 'dp', split_axis=0, concat_axis=0, tiled=True)  7.41 us
    all_to_all x1, starting transfers between devices, body(): back = lax.all_to_all(delta, 'dp', split_axis=0, concat_axis=0, tiled=True)  7.14 us
    dot_general x1, matrix products, body(): jnp.dot(attended, out_weight, preferred_element_type=jnp.float32)  5.97 us
    all_to_all x1, waiting for transfers between devices, body(): back = lax.all_to_all(delta, 'dp', split_axis=0, concat_axis=0, tiled=True)  5.27 us
  transfers between devices with their start and end apart: 4, of which 4 were waited for; matrix products, arithmetic and copies ran while one was open for 3% of the time, Pallas kernels for 0%

commit v1 on v0

--- a/solution.py
+++ b/solution.py
@@ -81,7 +81,8 @@
         slot_code[:, None] == jnp.arange(owners_count * capacity, dtype=jnp.int32)[None, :]
     ).astype(jnp.bfloat16)
     partial_value = jnp.dot(attended, out_weight, preferred_element_type=jnp.float32)
-    full = lax.psum(partial_value, "mp")
+    all_values = lax.all_gather(partial_value, "mp")
+    full = jnp.sum(all_values, axis=0)
     base = lax.dynamic_slice_in_dim(full, lax.axis_index("mp") * out_local, out_local, 1)
     got_rows = lax.all_to_all(send_rows, "dp", split_axis=0, concat_axis=0, tiled=True)
     got_ids = lax.all_to_all(send_ids, "dp", split_axis=0, concat_axis=0, tiled=True)

time: 118 us -> 218 us (1.85)
  waiting for transfers between devices: 25.1 us -> 115 us
  other arithmetic: 2.26 us -> 9.7 us
  blocking collectives: 34.2 us -> 36.4 us
    all_gather x0 -> x1, waiting for transfers between devices: none -> 105 us  [body(): all_values = lax.all_gather(partial_value, 'mp')]
    psum x1 -> x0, waiting for transfers between devices: 9.39 us -> none  [body(): full = lax.psum(partial_value, 'mp')]
    reduce_sum x0 -> x1, other arithmetic: none -> 7.43 us  [body(): full = jnp.sum(all_values, axis=0)]
    all_to_all x1, waiting for transfers between devices: 5.27 us -> 0.01 us  [body(): back = lax.all_to_all(delta, 'dp', split_axis=0, concat_axis=0, tiled=True)]
    psum x1, blocking collectives: 34.2 us -> 36.4 us  [body(): lax.psum(partial_value.reshape(owners_count * capacity, adapters_here * r...]
  transfers between devices with their start and end apart: 4 -> 4, of which waited for: 4 -> 3; matrix products, arithmetic and copies ran while one was open for 3% -> 5% of each run, Pallas kernels for 0% -> 0%
where the time goes in v1:
time: 218 us; the launch traced here: 216 us
  waiting for transfers between devices  115 us (53%)
  blocking collectives  36.4 us (17%)
  starting transfers between devices  22.2 us (10%)
  matrix products  17.7 us (8%)
  between operations  13.6 us (6%)
  other arithmetic  9.7 us (4%)
    all_gather x1, waiting for transfers between devices, body(): all_values = lax.all_gather(partial_value, 'mp')  105 us
    psum x1, blocking collectives, body(): lax.psum(partial_value.reshape(owners_count * capacity, adapters_here * r...  36.4 us
    all_to_all x1, waiting for transfers between devices, body(): lax.all_to_all(send_rows, 'dp', split_axis=0, concat_axis=0, tiled=True)  7.91 us
    all_to_all x1, starting transfers between devices, body(): lax.all_to_all(send_rows, 'dp', split_axis=0, concat_axis=0, tiled=True)  7.63 us
    reduce_sum x1, other arithmetic, body(): full = jnp.sum(all_values, axis=0)  7.43 us
    all_to_all x1, starting transfers between devices, body(): lax.all_to_all(send_ids, 'dp', split_axis=0, concat_axis=0, tiled=True)  7.41 us
    all_to_all x1, starting transfers between devices, body(): back = lax.all_to_all(delta, 'dp', split_axis=0, concat_axis=0, tiled=True)  7.14 us
    dot_general x1, matrix products, body(): jnp.dot(attended, out_weight, preferred_element_type=jnp.float32)  6.02 us
  transfers between devices with their start and end apart: 4, of which 3 were waited for; matrix products, arithmetic and copies ran while one was open for 5% of the time, Pallas kernels for 0%

profile of v1, /device:TPU:22, one launch (start us, length us, event | category | flops | bytes accessed | tf_op | source)
XLA Modules:
  0.0 216.3 jit_solution(15806310068035334202)
XLA Ops:
  6.5 0.0 copy-start
  6.5 0.0 copy-start.1
  6.5 0.0 copy-start.6
  6.5 0.0 copy-start.3
  6.5 0.0 all-gather.3.cloned.1.call-start
  6.6 0.8 iota_compare_fusion.6
  7.4 4.6 %fusion.42 = (f32[128,8]{1,0:T(8,128)S(1)}, f32[128,8,128]{2,1,0:T(8,128)S(1)}) fusion(bf16[128,8,128]{2,1,0:T(8,128)(2,1)} %param.12, bf16[128,1,128,128]{3,2,1,0:T(8,128)(2,1)} %param.13, pred[128,128]{1,0:T(8,128)(4,1)S(1)} %iota_compare_fusion.6), kind=kOutput, calls=%fused_computation.60 | convolution fusion | flops 33946624 | bytes 5001216 | tf_op jit(solution)/shard_map/bgjd,bgtd->bgjt/dot_general | solution.py:15
  12.0 0.1 copy.19
  12.1 0.0 copy-done.1
  12.1 0.0 copy-done.6
  12.1 0.3 fusion.36
  12.4 0.1 copy.20
  12.6 0.4 fusion.24
  13.0 0.1 copy.22
  13.1 0.1 copy.23
  13.2 0.0 copy-done.3
  13.3 3.5 %fusion.16 = bf16[128,8,128]{2,1,0:T(8,128)(2,1)S(1)} fusion(bf16[128,1,128,128]{3,2,1,0:T(8,128)(2,1)} %param.14, f32[128,8,128]{2,1,0:T(8,128)S(1)} %get-tuple-element.10, f32[128,128]{1,0:T(8,128)S(1)} %bitcast_convert_fusion, f32[128,8]{1,0:T(8,128)S(1)} %copy.23, f32[128,8]{1,0:T(8,128)S(1)} %copy.22, f32[128,8]{1,0:T(8,128)S(1)} %copy.20), kind=kOutput, calls=%fused_computation.14 | convolution fusion | flops 34340864 | bytes 5058560 | tf_op jit(solution)/shard_map/bgjt,bgtd->bgjd/dot_general | solution.py:29
  16.7 0.0 copy-start.4
  16.7 0.0 copy-start.5
  16.7 6.0 %fusion.26 = f32[128,4096]{1,0:T(8,128)} fusion(bf16[1024,4096]{1,0:T(8,128)(2,1)} %param.21, bf16[16,8,8,128]{3,2,1,0:T(8,128)(2,1)S(1)} %bitcast.77), kind=kOutput, calls=%fused_computation.25 | convolution fusion | flops 1073741824 | bytes 10747904 | tf_op jit(solution)/shard_map/dot_general | solution.py:83
  22.8 0.0 copy-start.2
  22.8 0.0 copy-start.7
  22.8 0.0 all-gather.3.cloned.1.call-update
  22.8 0.0 copy-done.4
  22.8 0.0 copy-done.5
  22.8 0.4 select_reduce_fusion
  23.3 0.1 fusion.35
  23.4 0.2 reduce_window_sum.11
  23.5 0.2 select_reduce_fusion.2
  23.7 0.1 select_reduce_fusion.1
  23.8 0.7 all_to_all.12
  24.5 7.4 %all-to-all-start = ((s32[32,1,8]{2,1,0:T(1,128)}), s32[32,1,8]{2,1,0:T(1,128)S(1)}, u32[]{:S(2)}, u32[]{:S(2)}) async-start(s32[32,1,8]{2,1,0:T(1,128)} %bitcast.7), calls=%async_computation | async-start | bytes 32768 | tf_op jit(solution)/shard_map/all_to_all | solution.py:88
  32.0 1.1 fusion.4
  33.0 2.5 %all-to-all-done = s32[32,1,8]{2,1,0:T(1,128)S(1)} async-done(((s32[32,1,8]{2,1,0:T(1,128)}), s32[32,1,8]{2,1,0:T(1,128)S(1)}, u32[]{:S(2)}, u32[]{:S(2)}) %all-to-all-start) | async-done | bytes 1056 | tf_op jit(solution)/shard_map/all_to_all | solution.py:88
  35.5 7.6 %all-to-all-start.1 = ((bf16[32,8,1024]{2,1,0:T(8,128)(2,1)}), bf16[32,8,1024]{2,1,0:T(8,128)(2,1)S(1)}, u32[]{:S(2)}, u32[]{:S(2)}) async-start(bf16[32,8,1024]{2,1,0:T(8,128)(2,1)} %fusion.4), calls=%async_computation.1 | async-start | bytes 1048576 | tf_op jit(solution)/shard_map/all_to_all | solution.py:87
  43.2 0.1 sub.34
  43.3 7.9 %all-to-all-done.1 = bf16[32,8,1024]{2,1,0:T(8,128)(2,1)S(1)} async-done(((bf16[32,8,1024]{2,1,0:T(8,128)(2,1)}), bf16[32,8,1024]{2,1,0:T(8,128)(2,1)S(1)}, u32[]{:S(2)}, u32[]{:S(2)}) %all-to-all-start.1) | async-done | bytes 524320 | tf_op jit(solution)/shard_map/all_to_all | solution.py:87
  51.2 0.0 copy-done
  51.2 0.3 fusion.22
  51.5 36.4 %all-reduce.1 = bf16[256,128]{0,1:T(8,128)(2,1)S(1)} all-reduce(f32[256,128]{0,1:T(8,128)S(1)} %bitcast.80), channel_id=1, replica_groups=mesh['dp'=32,'mp'=8] {'mp'}, use_global_device_ids=true, to_apply=%region_7.8 | all-reduce | flops 32768 | bytes 196608 | tf_op jit(solution)/shard_map/psum | solution.py:96
  88.0 0.0 copy-done.2
  88.0 1.0 fusion.19
  88.9 7.1 %all-to-all-start.2 = ((bf16[32,8,512]{2,1,0:T(8,128)(2,1)}), bf16[32,8,512]{2,1,0:T(8,128)(2,1)S(1)}, u32[]{:S(2)}, u32[]{:S(2)}) async-start(bf16[32,8,512]{2,1,0:T(8,128)(2,1)} %fusion.19), calls=%async_computation.2 | async-start | bytes 524288 | tf_op jit(solution)/shard_map/all_to_all | solution.py:102
  96.1 0.0 copy-done.7
  96.1 105.0 %all-gather.3.cloned.1.call-done = f32[1024,4096]{1,0:T(8,128)} async-done(((f32[128,4096]{1,0:T(8,128)}), f32[1024,4096]{1,0:T(8,128)}) %all-gather.3.cloned.1.call-update) | async-done | bytes 16777232 | tf_op jit(solution)/shard_map/all_gather | solution.py:84
  201.1 7.4 %reduce_sum.46 = f32[128,4096]{1,0:T(8,128)S(1)} reduce(f32[8,128,4096]{2,1,0:T(8,128)} %bitcast.76, f32[]{:T(128)} %constant.43.clone.1), dimensions={0}, to_apply=%region_2.3 | reduce | flops 3670016 | bytes 18874372 | tf_op jit(solution)/shard_map/reduce_sum | solution.py:85
  208.5 0.0 all-to-all-done.2
  208.5 0.9 fusion.21
  (11 shorter events, 0.2 us)
Async XLA Ops:
  6.5 44.7 %copy-start = (bf16[2,1024,64]{1,2,0:T(8,128)(2,1)S(1)}, bf16[2,1024,64]{1,2,0:T(8,128)(2,1)}, u32[]{:S(2)}) copy-start(bf16[2,1024,64]{1,2,0:T(8,128)(2,1)} %param.22) | copy-start | bytes 786436
  6.5 5.5 %copy-start.1 = (bf16[128,8,128]{2,1,0:T(8,128)(2,1)S(1)}, bf16[128,8,128]{2,1,0:T(8,128)(2,1)}, u32[]{:S(2)}) copy-start(bf16[128,8,128]{2,1,0:T(8,128)(2,1)} %param.12) | copy-start | bytes 786436
  6.5 5.5 %copy-start.6 = (bf16[128,1,128]{2,0,1:T(8,128)(2,1)S(1)}, bf16[128,1,128]{2,0,1:T(8,128)(2,1)}, u32[]{:S(2)}) copy-start(bf16[128,1,128]{2,0,1:T(8,128)(2,1)} %param.15) | copy-start | bytes 98308
  6.5 6.7 %copy-start.3 = (bf16[128,1,128]{2,0,1:T(8,128)(2,1)S(1)}, bf16[128,1,128]{2,0,1:T(8,128)(2,1)}, u32[]{:S(2)}) copy-start(bf16[128,1,128]{2,0,1:T(8,128)(2,1)} %param.16) | copy-start | bytes 98308
  6.5 194.5 %all-gather.3.cloned.1.call-start = ((), (), s32[]{:S(2)}) async-start(), calls=%async_computation.3 | async-start | bytes 18874368 | tf_op jit(solution)/shard_map/all_gather | solution.py:84
  16.7 6.1 %copy-start.4 = (s32[4096]{0:T(1024)S(1)}, s32[4096]{0:T(1024)}, u32[]{:S(2)}) copy-start(s32[4096]{0:T(1024)} %param.20) | copy-start | bytes 49156
  16.7 6.1 %copy-start.5 = (s32[128]{0:T(128)S(1)}, s32[128]{0:T(128)}, u32[]{:S(2)}) copy-start(s32[128]{0:T(128)} %param.19) | copy-start | bytes 1540
  22.8 65.2 %copy-start.2 = (bf16[2,64,512]{2,1,0:T(8,128)(2,1)S(1)}, bf16[2,64,512]{2,1,0:T(8,128)(2,1)}, u32[]{:S(2)}) copy-start(bf16[2,64,512]{2,1,0:T(8,128)(2,1)} %param.23) | copy-start | bytes 393220
  22.8 73.3 %copy-start.7 = (s32[128]{0:T(128)S(1)}, s32[128]{0:T(128)}, u32[]{:S(2)}) copy-start(s32[128]{0:T(128)} %param.18) | copy-start | bytes 1540
  24.5 11.0 %all-to-all-start = ((s32[32,1,8]{2,1,0:T(1,128)}), s32[32,1,8]{2,1,0:T(1,128)S(1)}, u32[]{:S(2)}, u32[]{:S(2)}) async-start(s32[32,1,8]{2,1,0:T(1,128)} %bitcast.7), calls=%async_computation | async-start | bytes 32768 | tf_op jit(solution)/shard_map/all_to_all | solution.py:88
  35.5 15.7 %all-to-all-start.1 = ((bf16[32,8,1024]{2,1,0:T(8,128)(2,1)}), bf16[32,8,1024]{2,1,0:T(8,128)(2,1)S(1)}, u32[]{:S(2)}, u32[]{:S(2)}) async-start(bf16[32,8,1024]{2,1,0:T(8,128)(2,1)} %fusion.4), calls=%async_computation.1 | async-start | bytes 1048576 | tf_op jit(solution)/shard_map/all_to_all | solution.py:87
  88.9 119.6 %all-to-all-start.2 = ((bf16[32,8,512]{2,1,0:T(8,128)(2,1)}), bf16[32,8,512]{2,1,0:T(8,128)(2,1)S(1)}, u32[]{:S(2)}, u32[]{:S(2)}) async-start(bf16[32,8,512]{2,1,0:T(8,128)(2,1)} %fusion.19), calls=%async_computation.2 | async-start | bytes 524288 | tf_op jit(solution)/shard_map/all_to_all | solution.py:102
Sparse Core Ops, SparseCore 0:
  22.9 178.1 all-gather.2
